TPU v7x, 128 devices: a whole 4x4x4 slice. The times are simulated.
128 devices in a mesh: dap: 128 (over x, y, z, core).
Axes of the slice: x: 4, y: 4, z: 4, core: 2. Of those that a mesh axis runs over, the one named last changes fastest.
Arguments:
- homolog_stack: float32 [256, 256, 256], P('dap'), may hold values from -5 to 5
- couple_tensor: float32 [256, 256, 128], P('dap'), may hold values from -6 to 6
- homolog_presence: int32 [256, 256], P('dap'), may hold values from 0 to 1
- amino_presence: int32 [256], replicated, may hold values 0 or 1
- horizontal_standard_factor: float32 [256], replicated, may hold values from 0.5 to 1.5
- horizontal_asking_matrix: bfloat16 [256, 256], replicated, may hold values from -7 to 7
- horizontal_lookup_triple: bfloat16 [256, 768], replicated, may hold values from -0.375 to 0.375
- horizontal_final_matrix: bfloat16 [256, 256], replicated, may hold values from -0.375 to 0.375
- couple_offset_factor: float32 [128], replicated, may hold values from 0.5 to 1.5
- couple_offset_matrix: bfloat16 [128, 8], replicated, may hold values from -2 to 2
- vertical_standard_factor: float32 [256], replicated, may hold values from 0.5 to 1.5
- vertical_asking_matrix: bfloat16 [256, 256], replicated, may hold values from -7 to 7
- vertical_lookup_triple: bfloat16 [256, 768], replicated, may hold values from -0.375 to 0.375
- vertical_final_matrix: bfloat16 [256, 256], replicated, may hold values from -0.375 to 0.375
- tensor_average_factor: float32 [256], replicated, may hold values from 0.5 to 1.5
- tensor_average_mapping: bfloat16 [256, 64], replicated, may hold values from -0.375 to 0.375
- tensor_average_final: bfloat16 [1024, 128], replicated, may hold values from -0.375 to 0.375
- trio_entry_factors: float32 [2, 128], replicated, may hold values from 0.5 to 1.5
- trio_flank_mappings: bfloat16 [2, 128, 512], replicated, may hold values from -0.5 to 0.5
- trio_final_switches: bfloat16 [2, 128, 128], replicated, may hold values from -0.5 to 0.5
- trio_multiplied_factors: float32 [2, 128], replicated, may hold values from 0.5 to 1.5
- trio_final_matrices: bfloat16 [2, 128, 128], replicated, may hold values from -1 to 1
Outputs:
- msa_out: float32 [256, 256, 256], P(None, 'dap')
- pair_out: float32 [256, 256, 128], P('dap')
All inputs are finite; a program needn't handle non-finite values.
Results may differ from a plain program's by a relative error of at most 0.015.
Values may be sent and summed in bfloat16 or wider, within the bound.
A program may use at most 64 MiB of HBM per device.

v0:
```python
import math

import jax
import jax.numpy as jnp
from jax import lax
from jax.experimental import pallas as pl
from jax.experimental.pallas import tpu as pltpu
from jax.sharding import PartitionSpec as P

N = 128
S = 256
H = 256
CZ = 128
HEADS = 8
WIDTH = 32
PLANE = 16
LINE = 8
BR = 40
EPS = 1e-05
PENALTY = 1e9
SCALE = 1.0 / math.sqrt(WIDTH)
F32, BF16 = jnp.float32, jnp.bfloat16
MESH = pl.DeviceIdType.MESH


def dot(a, b):
    return jnp.dot(a, b, preferred_element_type=F32)


def dot_nt(a, b):
    return lax.dot_general(a, b, (((1,), (1,)), ((), ())), preferred_element_type=F32)


def norm(x, gain, axis=-1):
    centred = x - jnp.mean(x, axis=axis, keepdims=True)
    spread = jnp.mean(centred * centred, axis=axis, keepdims=True)
    return centred * lax.rsqrt(spread + EPS) * gain


def send(src, dst, ssem, rsem, to):
    pltpu.make_async_remote_copy(
        src_ref=src, dst_ref=dst, send_sem=ssem, recv_sem=rsem, device_id=(to,), device_id_type=MESH
    ).start()


def landed(like, sem):
    pltpu.make_async_copy(like, like, sem).wait()


def every_other(halves, first):
    return jnp.concatenate([halves[c, pl.ds(first, 128, stride=2), :] for c in range(2)], axis=1)


def attend(q, k, v, o, bias, pens, heads_lane):
    o[...] = jnp.zeros_like(o)

    def head(h, _):
        sel = jnp.logical_and(heads_lane >= h * WIDTH, heads_lane < (h + 1) * WIDTH)
        only = sel.astype(F32).astype(BF16)
        for t in range(2):
            vm = v[t] * only
            for r in range(2):
                rows = slice(r * 128, (r + 1) * 128)
                scores = dot_nt(q[t, rows] * only, k[t])
                if bias is not None:
                    scores = scores + bias(h, r)
                scores = scores + pens[t]
                top = jnp.max(scores, axis=-1, keepdims=True)
                e = jnp.exp(scores - top)
                p = (e * (1.0 / jnp.sum(e, axis=-1, keepdims=True))).astype(BF16)
                o[t, rows] += dot(p, vm)
        return 0

    lax.fori_loop(0, HEADS, head, 0)


def body(
    msa, pair, pres, amino, g_row, wq1, wkvg1, wo1, g_bias, wb,
    g_col, wq2, wkvg2, wo2, g_opm, wlr, wfin, g_in, wproj, wgate, g_mid, wout,
    msa_out, pair_out,
    bsend, bg, b32, xn, msah, q, k, v, gate, o, a32, asend, arecv, xc, pm, pmt, cnt,
    lsend, rsend, lg, rg, r32, rp, lhs2, bd, osend, og, wt, wlrt, gmt, pad,
    t32, tsend, trecv, tgate, p32, psend, precv, pnow,
    ssem, rsem,
):
    me = lax.axis_index("dap")
    core = lax.rem(me, 2)
    partner = me + 1 - 2 * core
    chip = me // 2
    my_u, my_v = me // LINE, lax.rem(me, LINE)

    barrier = pltpu.get_barrier_semaphore()

    def hello(i, _):
        pl.semaphore_signal(
            barrier, inc=1, device_id=(lax.rem(me + i, N),), device_id_type=MESH
        )
        return 0

    lax.fori_loop(1, N, hello, 0)

    pad[...] = jnp.zeros_like(pad)
    pad[0:CZ, 0:HEADS] = wb[...].astype(F32)
    wbt = pad[0:CZ, :].T.astype(BF16)[0:16]
    for r in range(2):
        pn = norm(pair[r], g_bias[...][None, :]).astype(BF16)
        bt = dot_nt(wbt, pn)
        for j in range(2):
            at = (r * 2 + j) * 8
            bsend[at : at + 8, :] = bt[0:8, j * 128 : (j + 1) * 128].astype(BF16)
    pad[0:8, :] = jnp.zeros((8, 128), F32)
    presence = pres[...].astype(F32)
    for r in range(2):
        for j in range(2):
            pad[r * 2 + j : r * 2 + j + 1, :] = presence[r : r + 1, j * 128 : (j + 1) * 128]
    bsend[32:40, :] = pad[0:8, :].astype(BF16)
    bg[core, chip] = bsend[...]

    pl.semaphore_wait(barrier, N - 1)

    def spread_bias(i, _):
        to = lax.rem(me + 2 * i, N)
        send(bsend, bg.at[core, chip], ssem.at[0], rsem.at[0], to)
        return 0

    lax.fori_loop(1, N // 2, spread_bias, 0)

    lanes = lax.broadcasted_iota(jnp.int32, (1, H), 1)
    for s in range(2):
        x = norm(msa[s], g_row[...][None, :])
        for c in range(2):
            xn[c] = x[:, c * 128 : (c + 1) * 128]
            msah[s, c] = msa[s, :, c * 128 : (c + 1) * 128]
        xb = x.astype(BF16)
        k[s] = dot(xb, wkvg1[:, 0:H]).astype(BF16)
        v[s] = dot(xb, wkvg1[:, H : 2 * H]).astype(BF16)
        for r in range(2):
            rows = slice(r * 128, (r + 1) * 128)
            xr = every_other(xn, r).astype(BF16)
            q[s, rows] = (dot(xr, wq1[...]) * SCALE).astype(BF16)
            gate[s, rows] = jax.nn.sigmoid(dot(xr, wkvg1[:, 2 * H :]))

    for w in range(2):
        for c in range(4):
            cols = slice(c * 128, (c + 1) * 128)
            wt[w, cols, :] = wproj[w, :, cols].astype(F32).T.astype(BF16)
        gmt[w] = jnp.broadcast_to(g_mid[w : w + 1, :], (CZ, CZ)).T
    pad[:, 0:64] = wlr[...].astype(F32)
    wlrt[...] = pad[...].T.astype(BF16)[0:64]
    p32[...] = wfin[0:512, :].astype(F32)
    t32[0:512, :] = wfin[512:1024, :].astype(F32)
    bd[...] = jnp.zeros_like(bd)
    for b in range(32):
        part = jnp.concatenate(
            [p32[pl.ds(b, 16, stride=32), :], t32[pl.ds(b, 16, stride=32), :]], axis=0
        ).astype(BF16)
        for i in range(4):
            bd[b * 128 + i * 32 : b * 128 + (i + 1) * 32, i * 128 : (i + 1) * 128] = part

    landed(bg.at[0, pl.ds(0, N // 2 - 1)], rsem.at[0])
    send(bg.at[core], bg.at[core], ssem.at[1], rsem.at[1], partner)
    landed(bg.at[0], rsem.at[1])

    def widen(d, _):
        b32[pl.ds(pl.multiple_of(d * BR, 8), BR), :] = bg[lax.rem(d, 2), d // 2].astype(F32)
        return 0

    lax.fori_loop(0, N, widen, 0)

    def bias(h, r):
        return jnp.concatenate(
            [b32[pl.ds((r * 2 + j) * 8 + h, 128, stride=BR), :] for j in range(2)], axis=1
        )

    pens = [PENALTY * (presence[s : s + 1, :] - 1.0) for s in range(2)]
    attend(q, k, v, o, bias, pens, lanes)

    for s in range(2):
        for r in range(2):
            rows = slice(r * 128, (r + 1) * 128)
            y = (o[s, rows] * gate[s, rows]).astype(BF16)
            one = every_other(msah.at[s], r) + dot(y, wo1[...])
            for c in range(2):
                a32[pl.ds((s * 2 + r) * 2 + c, 128, stride=8), :] = one[:, c * 128 : (c + 1) * 128]
    asend[...] = a32[...].reshape(N, 8, 128).astype(BF16)
    arecv[me] = asend[me]

    def exchange(src, dst, sem):
        def one(i, _):
            to = lax.rem(me + i, N)
            send(src.at[to], dst.at[me], ssem.at[sem], rsem.at[sem], to)
            return 0

        lax.fori_loop(1, N, one, 0)

    def received(src, dst, sem):
        landed(dst.at[pl.ds(0, N - 1)], rsem.at[sem])
        landed(src.at[pl.ds(0, N - 1)], ssem.at[sem])

    exchange(asend, arecv, 2)

    for s in range(2):
        for j in range(2):
            pm[s * 128 : (s + 1) * 128, j * 128 : (j + 1) * 128] = b32[
                pl.ds(32 + s * 2 + j, 128, stride=BR), :
            ]
    pmt[...] = pm[...].T.astype(BF16)
    own = lax.broadcasted_iota(jnp.int32, (16, S), 0) + 2 * me
    hot = (lax.broadcasted_iota(jnp.int32, (16, S), 1) == own).astype(F32).astype(BF16)
    mine = dot(hot, pmt[...])
    pmb = pm[...].astype(BF16)
    for r in range(2):
        hot_c = (lax.broadcasted_iota(jnp.int32, (S, 128), 0) == 2 * me + r).astype(F32)
        col = dot(pmb, hot_c.astype(BF16)).astype(BF16)
        cnt[r] = 1.0 / jnp.maximum(dot(pmt[...], col), 1.0)

    received(asend, arecv, 2)
    a32[...] = arecv[...].astype(F32).reshape(N * 8, 128)
    for r in range(2):
        for s in range(2):
            for c in range(2):
                xc[r, s * 128 : (s + 1) * 128, c * 128 : (c + 1) * 128] = a32[
                    pl.ds((s * 2 + r) * 2 + c, 128, stride=8), :
                ]
        xb = norm(xc[r], g_col[...][None, :]).astype(BF16)
        q[r] = (dot(xb, wq2[...]) * SCALE).astype(BF16)
        k[r] = dot(xb, wkvg2[:, 0:H]).astype(BF16)
        v[r] = dot(xb, wkvg2[:, H : 2 * H]).astype(BF16)
        gate[r] = jax.nn.sigmoid(dot(xb, wkvg2[:, 2 * H :]))
    pens = [PENALTY * (mine[r : r + 1, :] - 1.0) for r in range(2)]
    attend(q, k, v, o, None, pens, lanes)
    for r in range(2):
        y = (o[r] * gate[r]).astype(BF16)
        done = xc[r] + dot(y, wo2[...])
        for s in range(2):
            for c in range(2):
                msa_out[pl.ds(s * 4 + c * 2 + r, 128, stride=8), :] = done[
                    s * 128 : (s + 1) * 128, c * 128 : (c + 1) * 128
                ]
        xb = norm(done, g_opm[...][None, :]).astype(BF16)
        halves = dot_nt(wlrt[...], xb) * mine[r : r + 1, :]
        lsend[r * 32 : (r + 1) * 32, :] = halves[0:32].astype(BF16)
        rsend[r * 32 : (r + 1) * 32, :] = halves[32:64].astype(BF16)

    lg[my_u] = lsend[...]
    rg[my_v] = rsend[...]

    def spread_left(i, _):
        send(lsend, lg.at[my_u], ssem.at[3], rsem.at[3], lax.rem(me + LINE * i, N))
        return 0

    def spread_right(i, _):
        to = my_u * LINE + lax.rem(my_v + i, LINE)
        send(rsend, rg.at[my_v], ssem.at[4], rsem.at[4], to)
        return 0

    lax.fori_loop(1, PLANE, spread_left, 0)
    lax.fori_loop(1, LINE, spread_right, 0)
    landed(rg.at[pl.ds(0, LINE - 1)], rsem.at[4])
    for c in range(2):
        r32[c] = rg[:, :, c * 128 : (c + 1) * 128].astype(F32).reshape(512, 128)
    for b in range(32):
        rp[b * 16 : (b + 1) * 16, :] = jnp.concatenate(
            [r32[c, pl.ds(b, 16, stride=32), :] for c in range(2)], axis=1
        ).astype(BF16)
    landed(lg.at[pl.ds(0, PLANE - 1)], rsem.at[3])
    for g in range(8):
        lb = lg[2 * g : 2 * g + 2].reshape(128, S)
        u = dot_nt(rp[...], lb).astype(BF16)
        for b in range(32):
            lhs2[g * 16 : (g + 1) * 16, b * 128 : (b + 1) * 128] = u[b * 16 : (b + 1) * 16]
    block = dot(lhs2[...], bd[...])
    for u in range(PLANE):
        for r in range(2):
            at = 2 * (u % 2) + r
            osend[u, r] = block[
                (u // 2) * 16 : (u // 2 + 1) * 16, at * 128 : (at + 1) * 128
            ].astype(BF16)
    og[my_u] = osend[my_u]

    def give_back(i, _):
        to_u = lax.rem(my_u + i, PLANE)
        send(osend.at[to_u], og.at[my_u], ssem.at[5], rsem.at[5], to_u * LINE + my_v)
        return 0

    lax.fori_loop(1, PLANE, give_back, 0)
    landed(og.at[pl.ds(0, PLANE - 1)], rsem.at[5])
    for r in range(2):
        delta = og[:, r].astype(F32).reshape(S, CZ)
        pnow[r] = pair[r] + delta * cnt[r]

    am = amino[...].astype(F32)[None, :]
    for w in range(2):
        for r in range(2):
            x = norm(pnow[r], g_in[w : w + 1, :]).astype(BF16)
            here = jnp.sum(jnp.where(lanes == 2 * me + r, am, 0.0), axis=-1, keepdims=True)
            mask = am * here
            pt = dot_nt(wt[w], x)
            for side in range(2):
                at = side * 256
                val = jax.nn.sigmoid(pt[at + 128 : at + 256]) * pt[at : at + 128] * mask
                for j in range(2):
                    t32[pl.ds(side * 4 + r * 2 + j, 128, stride=8), :] = val[
                        :, j * 128 : (j + 1) * 128
                    ]
            tgate[r] = jax.nn.sigmoid(dot(x, wgate[w]))
        tsend[w] = t32[...].reshape(N, 8, 128).astype(BF16)
        trecv[w, me] = tsend[w, me]
        exchange(tsend.at[w], trecv.at[w], 6 + 2 * w)
        received(tsend.at[w], trecv.at[w], 6 + 2 * w)
        t32[...] = trecv[w].astype(F32).reshape(N * 8, 128)
        sides = []
        for side in range(2):
            sides.append(
                jnp.concatenate(
                    [
                        jnp.concatenate(
                            [
                                t32[pl.ds(side * 4 + r * 2 + j, 128, stride=8), :]
                                for j in range(2)
                            ],
                            axis=1,
                        )
                        for r in range(2)
                    ],
                    axis=0,
                )
            )
        if w == 0:
            prod = dot_nt(sides[0].astype(BF16), sides[1].astype(BF16))
        else:
            prod = dot(sides[0].T.astype(BF16), sides[1].astype(BF16))
        for j in range(2):
            xn[j] = prod[:, j * 128 : (j + 1) * 128]
        for r in range(2):
            for j in range(2):
                rows = pl.ds(r * 128, 128) if w == 0 else pl.ds(r, 128, stride=2)
                p32[pl.ds(r * 2 + j, 128, stride=4), :] = xn[j, rows, :]
        psend[w] = p32[...].reshape(N, 4, 128).astype(BF16)
        precv[w, me] = psend[w, me]
        exchange(psend.at[w], precv.at[w], 7 + 2 * w)
        received(psend.at[w], precv.at[w], 7 + 2 * w)
        p32[...] = precv[w].astype(F32).reshape(N * 4, 128)
        for r in range(2):
            for j in range(2):
                pn = norm(p32[pl.ds(r * 2 + j, 128, stride=4), :], gmt[w], axis=0)
                update = dot(pn.T.astype(BF16), wout[w])
                rows = pl.ds(j, 128, stride=2) if w == 0 else pl.ds(j * 128, 128)
                new = pnow[r, rows, :] + update * tgate[r, rows, :]
                if w == 0:
                    pnow[r, rows, :] = new
                else:
                    pair_out[r, rows, :] = new

    landed(bg.at[0, pl.ds(0, N // 2 - 1)], ssem.at[0])
    landed(bg.at[0], ssem.at[1])
    landed(lg.at[pl.ds(0, PLANE - 1)], ssem.at[3])
    landed(rg.at[pl.ds(0, LINE - 1)], ssem.at[4])
    landed(og.at[pl.ds(0, PLANE - 1)], ssem.at[5])


SCRATCH = [
    ((BR, 128), BF16),
    ((2, N // 2, BR, 128), BF16),
    ((N * BR, 128), F32),
    ((2, S, 128), F32),
    ((2, 2, S, 128), F32),
    ((2, S, H), BF16),
    ((2, S, H), BF16),
    ((2, S, H), BF16),
    ((2, S, H), F32),
    ((2, S, H), F32),
    ((N * 8, 128), F32),
    ((N, 8, 128), BF16),
    ((N, 8, 128), BF16),
    ((2, S, H), F32),
    ((S, S), F32),
    ((S, S), BF16),
    ((2, S, CZ), F32),
    ((64, S), BF16),
    ((64, S), BF16),
    ((PLANE, 64, S), BF16),
    ((LINE, 64, S), BF16),
    ((2, 512, 128), F32),
    ((512, S), BF16),
    ((128, 4096), BF16),
    ((4096, 512), BF16),
    ((PLANE, 2, 16, 128), BF16),
    ((PLANE, 2, 16, 128), BF16),
    ((2, 512, 128), BF16),
    ((64, H), BF16),
    ((2, CZ, CZ), F32),
    ((H, 128), F32),
    ((N * 8, 128), F32),
    ((2, N, 8, 128), BF16),
    ((2, N, 8, 128), BF16),
    ((2, S, CZ), F32),
    ((N * 4, 128), F32),
    ((2, N, 4, 128), BF16),
    ((2, N, 4, 128), BF16),
    ((2, S, CZ), F32),
]


def shards(*args):
    vmem = pl.BlockSpec(memory_space=pltpu.VMEM)
    flat, pair = pl.pallas_call(
        body,
        out_shape=(
            jax.ShapeDtypeStruct((S * 4, 128), F32),
            jax.ShapeDtypeStruct((2, S, CZ), F32),
        ),
        in_specs=[vmem] * len(args),
        out_specs=(vmem, vmem),
        scratch_shapes=[pltpu.VMEM(shape, dtype) for shape, dtype in SCRATCH]
        + [pltpu.SemaphoreType.DMA((10,)), pltpu.SemaphoreType.DMA((10,))],
        compiler_params=pltpu.CompilerParams(
            collective_id=0, has_side_effects=True, vmem_limit_bytes=60 << 20
        ),
    )(*args)
    return flat.reshape(S, 2, 2, 128).transpose(0, 2, 1, 3).reshape(S, 2, H), pair


def solution(mesh):
    rows = P("dap", None, None)
    return jax.shard_map(
        shards,
        mesh=mesh,
        in_specs=(rows, rows, P("dap", None)) + (P(),) * 19,
        out_specs=(P(None, "dap", None), rows),
        check_vma=False,
    )
```

profile of v0, /device:TPU:1, one launch (start us, length us, event | category | flops | bytes accessed | tf_op | source)
XLA Modules:
  0.0 118.4 jit_solution(8066680913533014692)
XLA Ops:
  0.6 0.0 copy-start.1
  0.6 1.4 %copy.24.wb = bf16[128,8]{1,0:T(8,128)(2,1)} copy(bf16[128,8]{0,1:T(8,128)(2,1)} %param.31) | data formatting | bytes 4096 | tf_op args[9]
  2.0 0.0 copy-done.1
  2.0 0.7 copy.25.wlr
  2.8 112.8 %shard_map.221 = (f32[1024,128]{1,0:T(8,128)}, f32[2,256,128]{2,1,0:T(8,128)}) custom-call(f32[2,256,256]{2,1,0:T(8,128)} %msa.1, f32[2,256,128]{2,1,0:T(8,128)} %pair.1, s32[2,256]{1,0:T(2,128)} %pres.1, s32[256]{0:T(256)} %amino.1, f32[256]{0:T(256)} %g_row.1, bf16[256,256]{1,0:T(8,128)(2,1)} %wq1.1, bf16[256,768]{1,0:T(8,128)(2,1)} %wkvg1.1, ...), custom_call_target="tpu_custom_call" | custom-call | tf_op jit(solution)/shard_map/pallas_call | solution.py:407
  115.6 0.0 copy-start
  115.6 2.1 %copy.29 = f32[256,2,256]{2,1,0:T(2,128)} copy(f32[256,2,256]{2,1,0:T(2,128)} %bitcast.5) | data formatting | bytes 1048576
  117.7 0.0 copy-done
  117.7 0.7 copy.30
Async XLA Ops:
  0.6 1.4 %copy-start.1 = (bf16[256,64]{0,1:T(8,128)(2,1)S(1)}, bf16[256,64]{0,1:T(8,128)(2,1)}, u32[]{:S(2)}) copy-start(bf16[256,64]{0,1:T(8,128)(2,1)} %param.37) | copy-start | bytes 98308
  115.6 2.1 %copy-start = (f32[2,256,128]{2,1,0:T(8,128)S(1)}, f32[2,256,128]{2,1,0:T(8,128)}, u32[]{:S(2)}) copy-start(f32[2,256,128]{2,1,0:T(8,128)} %get-tuple-element.9) | copy-start | bytes 786436
where the time goes:
time: 119 us; the launch traced here: 118 us
  Pallas kernels  113 us (95%)
  local copies, waits for them, and re-layouts  4.9 us (4%)
    pallas_call x1, Pallas kernels, shards(): pl.pallas_call(body, out_shape=(jax.ShapeDtypeStruct((S * 4, 128), F32),...  113 us
    unnamed x8, local copies, waits for them, and re-layouts  4.9 us

commit v1 on v0

--- a/solution.py
+++ b/solution.py
@@ -15,7 +15,12 @@
 WIDTH = 32
 PLANE = 16
 LINE = 8
-BR = 40
+BA, BB = 24, 16
+HOPS = (0, 1, 2, 1)
+FAR_FIRST = sorted(
+    [(a, b, c) for a in range(4) for b in range(4) for c in range(4)],
+    key=lambda o: -(HOPS[o[0]] + HOPS[o[1]] + HOPS[o[2]]),
+)
 EPS = 1e-05
 PENALTY = 1e9
 SCALE = 1.0 / math.sqrt(WIDTH)
@@ -51,35 +56,36 @@
     return jnp.concatenate([halves[c, pl.ds(first, 128, stride=2), :] for c in range(2)], axis=1)
 
 
-def attend(q, k, v, o, bias, pens, heads_lane):
-    o[...] = jnp.zeros_like(o)
-
-    def head(h, _):
-        sel = jnp.logical_and(heads_lane >= h * WIDTH, heads_lane < (h + 1) * WIDTH)
-        only = sel.astype(F32).astype(BF16)
-        for t in range(2):
-            vm = v[t] * only
-            for r in range(2):
-                rows = slice(r * 128, (r + 1) * 128)
-                scores = dot_nt(q[t, rows] * only, k[t])
-                if bias is not None:
-                    scores = scores + bias(h, r)
-                scores = scores + pens[t]
-                top = jnp.max(scores, axis=-1, keepdims=True)
-                e = jnp.exp(scores - top)
-                p = (e * (1.0 / jnp.sum(e, axis=-1, keepdims=True))).astype(BF16)
-                o[t, rows] += dot(p, vm)
-        return 0
-
-    lax.fori_loop(0, HEADS, head, 0)
+def head_lanes(h):
+    lanes = lax.broadcasted_iota(jnp.int32, (1, H), 1)
+    return jnp.logical_and(lanes >= h * WIDTH, lanes < (h + 1) * WIDTH).astype(F32).astype(BF16)
+
+
+def spread_heads(v, vbd, t):
+    for h in range(HEADS):
+        vbd[t, h * S : (h + 1) * S, :] = v * head_lanes(h)
+
+
+def attend_head(h, q, kt, prob, bias, pens):
+    only = head_lanes(h)
+    for t in range(2):
+        scores = dot(q[t] * only, kt[t])
+        if bias is not None:
+            scores = scores + bias
+        scores = scores + pens[t]
+        top = jnp.max(scores, axis=-1, keepdims=True)
+        e = jnp.exp(scores - top)
+        prob[t, :, h * S : (h + 1) * S] = (
+            e * (1.0 / jnp.sum(e, axis=-1, keepdims=True))
+        ).astype(BF16)
 
 
 def body(
     msa, pair, pres, amino, g_row, wq1, wkvg1, wo1, g_bias, wb,
     g_col, wq2, wkvg2, wo2, g_opm, wlr, wfin, g_in, wproj, wgate, g_mid, wout,
     msa_out, pair_out,
-    bsend, bg, b32, xn, msah, q, k, v, gate, o, a32, asend, arecv, xc, pm, pmt, cnt,
-    lsend, rsend, lg, rg, r32, rp, lhs2, bd, osend, og, wt, wlrt, gmt, pad,
+    bsa, bsb, ba, bb, wa, wb32, xn, msah, q, kt, vbd, prob, gate, a32, asend, arecv, xc, pm, pmt, cnt,
+    lsend, rsend, lg, rg, r32, rp, lhs2, bd, osend, og, wt, gmt, pad,
     t32, tsend, trecv, tgate, p32, psend, precv, pnow,
     ssem, rsem,
 ):
@@ -89,51 +95,53 @@
     chip = me // 2
     my_u, my_v = me // LINE, lax.rem(me, LINE)
 
+    x_at, y_at, z_at = me // 32, lax.rem(me // 8, 4), lax.rem(chip, 4)
+
+    def chips():
+        for a, b, c in FAR_FIRST:
+            yield (
+                lax.rem(x_at + a, 4) * 16 + lax.rem(y_at + b, 4) * 4 + lax.rem(z_at + c, 4),
+                (a, b, c) == (0, 0, 0),
+            )
+
+    def peers():
+        for there, here in chips():
+            if not here:
+                yield there * 2 + core
+            yield there * 2 + 1 - core
+
     barrier = pltpu.get_barrier_semaphore()
-
-    def hello(i, _):
-        pl.semaphore_signal(
-            barrier, inc=1, device_id=(lax.rem(me + i, N),), device_id_type=MESH
-        )
-        return 0
-
-    lax.fori_loop(1, N, hello, 0)
-
+    for to in peers():
+        pl.semaphore_signal(barrier, inc=1, device_id=(to,), device_id_type=MESH)
+
+    wbt = wb[...]
     pad[...] = jnp.zeros_like(pad)
-    pad[0:CZ, 0:HEADS] = wb[...].astype(F32)
-    wbt = pad[0:CZ, :].T.astype(BF16)[0:16]
     for r in range(2):
         pn = norm(pair[r], g_bias[...][None, :]).astype(BF16)
         bt = dot_nt(wbt, pn)
         for j in range(2):
-            at = (r * 2 + j) * 8
-            bsend[at : at + 8, :] = bt[0:8, j * 128 : (j + 1) * 128].astype(BF16)
-    pad[0:8, :] = jnp.zeros((8, 128), F32)
+            cols = slice(j * 128, (j + 1) * 128)
+            at = (r * 2 + j) * 4
+            pad[at : at + 4, :] = bt[0:4, cols]
+            pad[BA + at : BA + at + 4, :] = bt[4:8, cols]
     presence = pres[...].astype(F32)
     for r in range(2):
         for j in range(2):
-            pad[r * 2 + j : r * 2 + j + 1, :] = presence[r : r + 1, j * 128 : (j + 1) * 128]
-    bsend[32:40, :] = pad[0:8, :].astype(BF16)
-    bg[core, chip] = bsend[...]
-
-    pl.semaphore_wait(barrier, N - 1)
-
-    def spread_bias(i, _):
-        to = lax.rem(me + 2 * i, N)
-        send(bsend, bg.at[core, chip], ssem.at[0], rsem.at[0], to)
-        return 0
-
-    lax.fori_loop(1, N // 2, spread_bias, 0)
-
-    lanes = lax.broadcasted_iota(jnp.int32, (1, H), 1)
+            at = 16 + r * 2 + j
+            pad[at : at + 1, :] = presence[r : r + 1, j * 128 : (j + 1) * 128]
+    bsa[...] = pad[0:BA, :].astype(BF16)
+    bsb[...] = pad[BA : BA + BB, :].astype(BF16)
+    ba[core, chip] = bsa[...]
+    bb[core, chip] = bsb[...]
+
     for s in range(2):
         x = norm(msa[s], g_row[...][None, :])
         for c in range(2):
             xn[c] = x[:, c * 128 : (c + 1) * 128]
             msah[s, c] = msa[s, :, c * 128 : (c + 1) * 128]
         xb = x.astype(BF16)
-        k[s] = dot(xb, wkvg1[:, 0:H]).astype(BF16)
-        v[s] = dot(xb, wkvg1[:, H : 2 * H]).astype(BF16)
+        kt[s] = dot(xb, wkvg1[:, 0:H]).T.astype(BF16)
+        spread_heads(dot(xb, wkvg1[:, H : 2 * H]).astype(BF16), vbd, s)
         for r in range(2):
             rows = slice(r * 128, (r + 1) * 128)
             xr = every_other(xn, r).astype(BF16)
@@ -145,8 +153,6 @@
             cols = slice(c * 128, (c + 1) * 128)
             wt[w, cols, :] = wproj[w, :, cols].astype(F32).T.astype(BF16)
         gmt[w] = jnp.broadcast_to(g_mid[w : w + 1, :], (CZ, CZ)).T
-    pad[:, 0:64] = wlr[...].astype(F32)
-    wlrt[...] = pad[...].T.astype(BF16)[0:64]
     p32[...] = wfin[0:512, :].astype(F32)
     t32[0:512, :] = wfin[512:1024, :].astype(F32)
     bd[...] = jnp.zeros_like(bd)
@@ -157,41 +163,49 @@
         for i in range(4):
             bd[b * 128 + i * 32 : b * 128 + (i + 1) * 32, i * 128 : (i + 1) * 128] = part
 
-    landed(bg.at[0, pl.ds(0, N // 2 - 1)], rsem.at[0])
-    send(bg.at[core], bg.at[core], ssem.at[1], rsem.at[1], partner)
-    landed(bg.at[0], rsem.at[1])
-
-    def widen(d, _):
-        b32[pl.ds(pl.multiple_of(d * BR, 8), BR), :] = bg[lax.rem(d, 2), d // 2].astype(F32)
-        return 0
-
-    lax.fori_loop(0, N, widen, 0)
-
-    def bias(h, r):
-        return jnp.concatenate(
-            [b32[pl.ds((r * 2 + j) * 8 + h, 128, stride=BR), :] for j in range(2)], axis=1
-        )
+    pl.semaphore_wait(barrier, N - 1)
+    for src, dst, sem in ((bsa, ba, 0), (bsb, bb, 10)):
+        for there, here in chips():
+            if not here:
+                send(src, dst.at[core, chip], ssem.at[sem], rsem.at[sem], there * 2 + core)
 
     pens = [PENALTY * (presence[s : s + 1, :] - 1.0) for s in range(2)]
-    attend(q, k, v, o, bias, pens, lanes)
-
+    for half, (dst, wide, rows_of, sem) in enumerate(((ba, wa, BA, 0), (bb, wb32, BB, 10))):
+        landed(dst.at[0, pl.ds(0, N // 2 - 1)], rsem.at[sem])
+        send(dst.at[core], dst.at[core], ssem.at[sem + 1], rsem.at[sem + 1], partner)
+        landed(dst.at[0], rsem.at[sem + 1])
+        landed(dst.at[0, pl.ds(0, N // 2 - 1)], ssem.at[sem])
+        landed(dst.at[0], ssem.at[sem + 1])
+        for d in range(N):
+            wide[d * rows_of : (d + 1) * rows_of, :] = dst[d % 2, d // 2].astype(F32)
+        for h in range(4):
+            bias = jnp.concatenate(
+                [
+                    jnp.concatenate(
+                        [
+                            wide[pl.ds((r * 2 + j) * 4 + h, 128, stride=rows_of), :]
+                            for j in range(2)
+                        ],
+                        axis=1,
+                    )
+                    for r in range(2)
+                ],
+                axis=0,
+            )
+            attend_head(half * 4 + h, q, kt, prob, bias, pens)
     for s in range(2):
-        for r in range(2):
-            rows = slice(r * 128, (r + 1) * 128)
-            y = (o[s, rows] * gate[s, rows]).astype(BF16)
-            one = every_other(msah.at[s], r) + dot(y, wo1[...])
+        y = (dot(prob[s], vbd[s]) * gate[s]).astype(BF16)
+        step = dot(y, wo1[...])
+        for r in range(2):
+            one = every_other(msah.at[s], r) + step[r * 128 : (r + 1) * 128]
             for c in range(2):
                 a32[pl.ds((s * 2 + r) * 2 + c, 128, stride=8), :] = one[:, c * 128 : (c + 1) * 128]
     asend[...] = a32[...].reshape(N, 8, 128).astype(BF16)
     arecv[me] = asend[me]
 
     def exchange(src, dst, sem):
-        def one(i, _):
-            to = lax.rem(me + i, N)
+        for to in peers():
             send(src.at[to], dst.at[me], ssem.at[sem], rsem.at[sem], to)
-            return 0
-
-        lax.fori_loop(1, N, one, 0)
 
     def received(src, dst, sem):
         landed(dst.at[pl.ds(0, N - 1)], rsem.at[sem])
@@ -201,8 +215,8 @@
 
     for s in range(2):
         for j in range(2):
-            pm[s * 128 : (s + 1) * 128, j * 128 : (j + 1) * 128] = b32[
-                pl.ds(32 + s * 2 + j, 128, stride=BR), :
+            pm[s * 128 : (s + 1) * 128, j * 128 : (j + 1) * 128] = wa[
+                pl.ds(16 + s * 2 + j, 128, stride=BA), :
             ]
     pmt[...] = pm[...].T.astype(BF16)
     own = lax.broadcasted_iota(jnp.int32, (16, S), 0) + 2 * me
@@ -224,13 +238,14 @@
                 ]
         xb = norm(xc[r], g_col[...][None, :]).astype(BF16)
         q[r] = (dot(xb, wq2[...]) * SCALE).astype(BF16)
-        k[r] = dot(xb, wkvg2[:, 0:H]).astype(BF16)
-        v[r] = dot(xb, wkvg2[:, H : 2 * H]).astype(BF16)
+        kt[r] = dot(xb, wkvg2[:, 0:H]).T.astype(BF16)
+        spread_heads(dot(xb, wkvg2[:, H : 2 * H]).astype(BF16), vbd, r)
         gate[r] = jax.nn.sigmoid(dot(xb, wkvg2[:, 2 * H :]))
     pens = [PENALTY * (mine[r : r + 1, :] - 1.0) for r in range(2)]
-    attend(q, k, v, o, None, pens, lanes)
-    for r in range(2):
-        y = (o[r] * gate[r]).astype(BF16)
+    for h in range(HEADS):
+        attend_head(h, q, kt, prob, None, pens)
+    for r in range(2):
+        y = (dot(prob[r], vbd[r]) * gate[r]).astype(BF16)
         done = xc[r] + dot(y, wo2[...])
         for s in range(2):
             for c in range(2):
@@ -238,7 +253,7 @@
                     s * 128 : (s + 1) * 128, c * 128 : (c + 1) * 128
                 ]
         xb = norm(done, g_opm[...][None, :]).astype(BF16)
-        halves = dot_nt(wlrt[...], xb) * mine[r : r + 1, :]
+        halves = dot_nt(wlr[...], xb) * mine[r : r + 1, :]
         lsend[r * 32 : (r + 1) * 32, :] = halves[0:32].astype(BF16)
         rsend[r * 32 : (r + 1) * 32, :] = halves[32:64].astype(BF16)
 
@@ -264,6 +279,8 @@
             [r32[c, pl.ds(b, 16, stride=32), :] for c in range(2)], axis=1
         ).astype(BF16)
     landed(lg.at[pl.ds(0, PLANE - 1)], rsem.at[3])
+    landed(lg.at[pl.ds(0, PLANE - 1)], ssem.at[3])
+    landed(rg.at[pl.ds(0, LINE - 1)], ssem.at[4])
     for g in range(8):
         lb = lg[2 * g : 2 * g + 2].reshape(128, S)
         u = dot_nt(rp[...], lb).astype(BF16)
@@ -285,10 +302,12 @@
 
     lax.fori_loop(1, PLANE, give_back, 0)
     landed(og.at[pl.ds(0, PLANE - 1)], rsem.at[5])
+    landed(og.at[pl.ds(0, PLANE - 1)], ssem.at[5])
     for r in range(2):
         delta = og[:, r].astype(F32).reshape(S, CZ)
         pnow[r] = pair[r] + delta * cnt[r]
 
+    lanes = lax.broadcasted_iota(jnp.int32, (1, S), 1)
     am = amino[...].astype(F32)[None, :]
     for w in range(2):
         for r in range(2):
@@ -352,23 +371,20 @@
                 else:
                     pair_out[r, rows, :] = new
 
-    landed(bg.at[0, pl.ds(0, N // 2 - 1)], ssem.at[0])
-    landed(bg.at[0], ssem.at[1])
-    landed(lg.at[pl.ds(0, PLANE - 1)], ssem.at[3])
-    landed(rg.at[pl.ds(0, LINE - 1)], ssem.at[4])
-    landed(og.at[pl.ds(0, PLANE - 1)], ssem.at[5])
-
 
 SCRATCH = [
-    ((BR, 128), BF16),
-    ((2, N // 2, BR, 128), BF16),
-    ((N * BR, 128), F32),
+    ((BA, 128), BF16),
+    ((BB, 128), BF16),
+    ((2, N // 2, BA, 128), BF16),
+    ((2, N // 2, BB, 128), BF16),
+    ((N * BA, 128), F32),
+    ((N * BB, 128), F32),
     ((2, S, 128), F32),
     ((2, 2, S, 128), F32),
     ((2, S, H), BF16),
-    ((2, S, H), BF16),
-    ((2, S, H), BF16),
-    ((2, S, H), F32),
+    ((2, H, S), BF16),
+    ((2, HEADS * S, H), BF16),
+    ((2, S, HEADS * S), BF16),
     ((2, S, H), F32),
     ((N * 8, 128), F32),
     ((N, 8, 128), BF16),
@@ -388,9 +404,8 @@
     ((PLANE, 2, 16, 128), BF16),
     ((PLANE, 2, 16, 128), BF16),
     ((2, 512, 128), BF16),
-    ((64, H), BF16),
     ((2, CZ, CZ), F32),
-    ((H, 128), F32),
+    ((BA + BB, 128), F32),
     ((N * 8, 128), F32),
     ((2, N, 8, 128), BF16),
     ((2, N, 8, 128), BF16),
@@ -413,11 +428,11 @@
         in_specs=[vmem] * len(args),
         out_specs=(vmem, vmem),
         scratch_shapes=[pltpu.VMEM(shape, dtype) for shape, dtype in SCRATCH]
-        + [pltpu.SemaphoreType.DMA((10,)), pltpu.SemaphoreType.DMA((10,))],
+        + [pltpu.SemaphoreType.DMA((12,)), pltpu.SemaphoreType.DMA((12,))],
         compiler_params=pltpu.CompilerParams(
             collective_id=0, has_side_effects=True, vmem_limit_bytes=60 << 20
         ),
-    )(*args)
+    )(*args[:9], args[9].T, *args[10:15], args[15].T, *args[16:])
     return flat.reshape(S, 2, 2, 128).transpose(0, 2, 1, 3).reshape(S, 2, H), pair
 
 

time: 119 us -> 85.6 us (0.72)
  Pallas kernels: 113 us -> 82 us
  local copies, waits for them, and re-layouts: 4.9 us -> 2.76 us
    pallas_call x1, Pallas kernels: 113 us -> 82 us  [shards(): pl.pallas_call(body, out_shape=(jax.ShapeDtypeStruct((S * 4, 128), F32),...]
    unnamed x8 -> x4, local copies, waits for them, and re-layouts: 4.9 us -> 2.76 us
where the time goes in v1:
time: 85.6 us; the launch traced here: 85.4 us
  Pallas kernels  82 us (96%)
  local copies, waits for them, and re-layouts  2.76 us (3%)
    pallas_call x1, Pallas kernels, shards(): pl.pallas_call(body, out_shape=(jax.ShapeDtypeStruct((S * 4, 128), F32),...  82 us
    unnamed x4, local copies, waits for them, and re-layouts  2.76 us

profile of v1, /device:TPU:1, one launch (start us, length us, event | category | flops | bytes accessed | tf_op | source)
XLA Modules:
  0.0 85.4 jit_solution(93966081022861816)
XLA Ops:
  0.6 82.0 %shard_map.221 = (f32[1024,128]{1,0:T(8,128)}, f32[2,256,128]{2,1,0:T(8,128)}) custom-call(f32[2,256,256]{2,1,0:T(8,128)} %msa.1, f32[2,256,128]{2,1,0:T(8,128)} %pair.1, s32[2,256]{1,0:T(2,128)} %pres.1, s32[256]{0:T(256)} %amino.1, f32[256]{0:T(256)} %g_row.1, bf16[256,256]{1,0:T(8,128)(2,1)} %wq1.1, bf16[256,768]{1,0:T(8,128)(2,1)} %wkvg1.1, ...), custom_call_target="tpu_custom_call" | custom-call | tf_op jit(solution)/shard_map/pallas_call | solution.py:422
  82.6 0.0 copy-start
  82.7 2.1 %copy.27 = f32[256,2,256]{2,1,0:T(2,128)} copy(f32[256,2,256]{2,1,0:T(2,128)} %bitcast.7) | data formatting | bytes 1048576
  84.7 0.0 copy-done
  84.7 0.7 copy.28
Async XLA Ops:
  82.6 2.1 %copy-start = (f32[2,256,128]{2,1,0:T(8,128)S(1)}, f32[2,256,128]{2,1,0:T(8,128)}, u32[]{:S(2)}) copy-start(f32[2,256,128]{2,1,0:T(8,128)} %get-tuple-element.9) | copy-start | bytes 786436

commit v2 on v1

--- a/solution.py
+++ b/solution.py
@@ -15,12 +15,14 @@
 WIDTH = 32
 PLANE = 16
 LINE = 8
-BA, BB = 24, 16
+BA, BB = 16, 24
+N_IN = 22
 HOPS = (0, 1, 2, 1)
 FAR_FIRST = sorted(
     [(a, b, c) for a in range(4) for b in range(4) for c in range(4)],
     key=lambda o: -(HOPS[o[0]] + HOPS[o[1]] + HOPS[o[2]]),
 )
+PLANE_FAR_FIRST = sorted(range(1, 16), key=lambda n: -(HOPS[n // 4] + HOPS[n % 4]))
 EPS = 1e-05
 PENALTY = 1e9
 SCALE = 1.0 / math.sqrt(WIDTH)
@@ -66,29 +68,29 @@
         vbd[t, h * S : (h + 1) * S, :] = v * head_lanes(h)
 
 
-def attend_head(h, q, kt, prob, bias, pens):
-    only = head_lanes(h)
-    for t in range(2):
-        scores = dot(q[t] * only, kt[t])
-        if bias is not None:
-            scores = scores + bias
-        scores = scores + pens[t]
-        top = jnp.max(scores, axis=-1, keepdims=True)
-        e = jnp.exp(scores - top)
-        prob[t, :, h * S : (h + 1) * S] = (
-            e * (1.0 / jnp.sum(e, axis=-1, keepdims=True))
-        ).astype(BF16)
-
-
-def body(
-    msa, pair, pres, amino, g_row, wq1, wkvg1, wo1, g_bias, wb,
-    g_col, wq2, wkvg2, wo2, g_opm, wlr, wfin, g_in, wproj, wgate, g_mid, wout,
-    msa_out, pair_out,
-    bsa, bsb, ba, bb, wa, wb32, xn, msah, q, kt, vbd, prob, gate, a32, asend, arecv, xc, pm, pmt, cnt,
-    lsend, rsend, lg, rg, r32, rp, lhs2, bd, osend, og, wt, gmt, pad,
-    t32, tsend, trecv, tgate, p32, psend, precv, pnow,
-    ssem, rsem,
-):
+def attend_head(h, t, q, kt, prob, bias, pen):
+    scores = dot(q[t] * head_lanes(h), kt[t])
+    if bias is not None:
+        scores = scores + bias
+    scores = scores + pen
+    top = jnp.max(scores, axis=-1, keepdims=True)
+    e = jnp.exp(scores - top)
+    prob[t, :, h * S : (h + 1) * S] = (e * (1.0 / jnp.sum(e, axis=-1, keepdims=True))).astype(BF16)
+
+
+def body(*refs):
+    ins, outs, refs = refs[:N_IN], refs[N_IN : N_IN + 2], refs[N_IN + 2 :]
+    here, refs = refs[:N_IN], refs[N_IN:]
+    (
+        msa, pair, pres, amino, g_row, wq1, wkvg1, wo1, g_bias, wb, g_col,
+        wq2, wkvg2, wo2, g_opm, wlr, wfin, g_in, wproj, wgate, g_mid, wout,
+    ) = here
+    (
+        msa_out, pair_out, bsa, bsb, ba, bb, wa, wb32, xn, msah, q, kt, vbd, prob, gate, a32,
+        asend, arecv, xc, pm, pmt, cnt, lsend, rsend, lg, rg, r32, rp, lhs2, bd, osend, og,
+        wt, gmt, pad, t32, tsend, trecv, tgate, p32, psend, precv, pnow,
+        ssem, rsem, isem, osem,
+    ) = refs
     me = lax.axis_index("dap")
     core = lax.rem(me, 2)
     partner = me + 1 - 2 * core
@@ -114,10 +116,19 @@
     for to in peers():
         pl.semaphore_signal(barrier, inc=1, device_id=(to,), device_id_type=MESH)
 
+    order = (1, 8, 9, 2, 0, 4, 5, 6, 18, 20, 16, 7, 3, 10, 11, 12, 13, 14, 15, 17, 19, 21)
+    for n in order:
+        pltpu.make_async_copy(ins[n], here[n], isem.at[n]).start()
+
+    def arrived(*which):
+        for n in which:
+            pltpu.make_async_copy(ins[n], here[n], isem.at[n]).wait()
+
+    arrived(1, 8, 9, 2)
     wbt = wb[...]
     pad[...] = jnp.zeros_like(pad)
     for r in range(2):
-        pn = norm(pair[r], g_bias[...][None, :]).astype(BF16)
+        pn = norm(pair[r], g_bias[...]).astype(BF16)
         bt = dot_nt(wbt, pn)
         for j in range(2):
             cols = slice(j * 128, (j + 1) * 128)
@@ -127,15 +138,16 @@
     presence = pres[...].astype(F32)
     for r in range(2):
         for j in range(2):
-            at = 16 + r * 2 + j
+            at = BA + 16 + r * 2 + j
             pad[at : at + 1, :] = presence[r : r + 1, j * 128 : (j + 1) * 128]
     bsa[...] = pad[0:BA, :].astype(BF16)
     bsb[...] = pad[BA : BA + BB, :].astype(BF16)
     ba[core, chip] = bsa[...]
     bb[core, chip] = bsb[...]
 
+    arrived(0, 4, 5, 6)
     for s in range(2):
-        x = norm(msa[s], g_row[...][None, :])
+        x = norm(msa[s], g_row[...])
         for c in range(2):
             xn[c] = x[:, c * 128 : (c + 1) * 128]
             msah[s, c] = msa[s, :, c * 128 : (c + 1) * 128]
@@ -148,6 +160,7 @@
             q[s, rows] = (dot(xr, wq1[...]) * SCALE).astype(BF16)
             gate[s, rows] = jax.nn.sigmoid(dot(xr, wkvg1[:, 2 * H :]))
 
+    arrived(18, 20, 16, 7, 3, 10, 11, 12, 13, 14, 15, 17, 19, 21)
     for w in range(2):
         for c in range(4):
             cols = slice(c * 128, (c + 1) * 128)
@@ -170,9 +183,14 @@
                 send(src, dst.at[core, chip], ssem.at[sem], rsem.at[sem], there * 2 + core)
 
     pens = [PENALTY * (presence[s : s + 1, :] - 1.0) for s in range(2)]
-    for half, (dst, wide, rows_of, sem) in enumerate(((ba, wa, BA, 0), (bb, wb32, BB, 10))):
+    halves = ((ba, wa, BA, 0), (bb, wb32, BB, 10))
+
+    def swap(dst, sem):
         landed(dst.at[0, pl.ds(0, N // 2 - 1)], rsem.at[sem])
         send(dst.at[core], dst.at[core], ssem.at[sem + 1], rsem.at[sem + 1], partner)
+
+    swap(ba, 0)
+    for half, (dst, wide, rows_of, sem) in enumerate(halves):
         landed(dst.at[0], rsem.at[sem + 1])
         landed(dst.at[0, pl.ds(0, N // 2 - 1)], ssem.at[sem])
         landed(dst.at[0], ssem.at[sem + 1])
@@ -192,7 +210,10 @@
                 ],
                 axis=0,
             )
-            attend_head(half * 4 + h, q, kt, prob, bias, pens)
+            for t in range(2):
+                attend_head(half * 4 + h, t, q, kt, prob, bias, pens[t])
+            if half == 0 and h == 1:
+                swap(bb, 10)
     for s in range(2):
         y = (dot(prob[s], vbd[s]) * gate[s]).astype(BF16)
         step = dot(y, wo1[...])
@@ -215,8 +236,8 @@
 
     for s in range(2):
         for j in range(2):
-            pm[s * 128 : (s + 1) * 128, j * 128 : (j + 1) * 128] = wa[
-                pl.ds(16 + s * 2 + j, 128, stride=BA), :
+            pm[s * 128 : (s + 1) * 128, j * 128 : (j + 1) * 128] = wb32[
+                pl.ds(16 + s * 2 + j, 128, stride=BB), :
             ]
     pmt[...] = pm[...].T.astype(BF16)
     own = lax.broadcasted_iota(jnp.int32, (16, S), 0) + 2 * me
@@ -236,15 +257,14 @@
                 xc[r, s * 128 : (s + 1) * 128, c * 128 : (c + 1) * 128] = a32[
                     pl.ds((s * 2 + r) * 2 + c, 128, stride=8), :
                 ]
-        xb = norm(xc[r], g_col[...][None, :]).astype(BF16)
+        xb = norm(xc[r], g_col[...]).astype(BF16)
         q[r] = (dot(xb, wq2[...]) * SCALE).astype(BF16)
         kt[r] = dot(xb, wkvg2[:, 0:H]).T.astype(BF16)
         spread_heads(dot(xb, wkvg2[:, H : 2 * H]).astype(BF16), vbd, r)
         gate[r] = jax.nn.sigmoid(dot(xb, wkvg2[:, 2 * H :]))
-    pens = [PENALTY * (mine[r : r + 1, :] - 1.0) for r in range(2)]
-    for h in range(HEADS):
-        attend_head(h, q, kt, prob, None, pens)
-    for r in range(2):
+    for r in range(2):
+        for h in range(HEADS):
+            attend_head(h, r, q, kt, prob, None, PENALTY * (mine[r : r + 1, :] - 1.0))
         y = (dot(prob[r], vbd[r]) * gate[r]).astype(BF16)
         done = xc[r] + dot(y, wo2[...])
         for s in range(2):
@@ -252,55 +272,50 @@
                 msa_out[pl.ds(s * 4 + c * 2 + r, 128, stride=8), :] = done[
                     s * 128 : (s + 1) * 128, c * 128 : (c + 1) * 128
                 ]
-        xb = norm(done, g_opm[...][None, :]).astype(BF16)
-        halves = dot_nt(wlr[...], xb) * mine[r : r + 1, :]
-        lsend[r * 32 : (r + 1) * 32, :] = halves[0:32].astype(BF16)
-        rsend[r * 32 : (r + 1) * 32, :] = halves[32:64].astype(BF16)
-
-    lg[my_u] = lsend[...]
-    rg[my_v] = rsend[...]
-
-    def spread_left(i, _):
-        send(lsend, lg.at[my_u], ssem.at[3], rsem.at[3], lax.rem(me + LINE * i, N))
-        return 0
-
-    def spread_right(i, _):
-        to = my_u * LINE + lax.rem(my_v + i, LINE)
-        send(rsend, rg.at[my_v], ssem.at[4], rsem.at[4], to)
-        return 0
-
-    lax.fori_loop(1, PLANE, spread_left, 0)
-    lax.fori_loop(1, LINE, spread_right, 0)
+        xb = norm(done, g_opm[...]).astype(BF16)
+        projected = dot_nt(wlr[...], xb) * mine[r : r + 1, :]
+        lsend[r] = projected[0:32].astype(BF16)
+        rsend[r] = projected[32:64].astype(BF16)
+        lg[r, my_u] = lsend[r]
+        if r == 1:
+            rg[my_v] = rsend[...]
+            for n in range(1, LINE):
+                send(
+                    rsend, rg.at[my_v], ssem.at[4], rsem.at[4],
+                    my_u * LINE + lax.rem(my_v + n, LINE),
+                )
+        for n in PLANE_FAR_FIRST:
+            to = lax.rem(x_at + n // 4, 4) * 32 + lax.rem(y_at + n % 4, 4) * 8 + my_v
+            send(lsend.at[r], lg.at[r, my_u], ssem.at[3 + 9 * r], rsem.at[3 + 9 * r], to)
+    pltpu.make_async_copy(msa_out, outs[0], osem.at[0]).start()
+
     landed(rg.at[pl.ds(0, LINE - 1)], rsem.at[4])
     for c in range(2):
-        r32[c] = rg[:, :, c * 128 : (c + 1) * 128].astype(F32).reshape(512, 128)
+        r32[c] = rg[:, :, :, c * 128 : (c + 1) * 128].astype(F32).reshape(512, 128)
     for b in range(32):
         rp[b * 16 : (b + 1) * 16, :] = jnp.concatenate(
             [r32[c, pl.ds(b, 16, stride=32), :] for c in range(2)], axis=1
         ).astype(BF16)
-    landed(lg.at[pl.ds(0, PLANE - 1)], rsem.at[3])
-    landed(lg.at[pl.ds(0, PLANE - 1)], ssem.at[3])
+    for r in range(2):
+        for sems in (rsem, ssem):
+            landed(lg.at[0, pl.ds(0, PLANE - 1)], sems.at[3 + 9 * r])
+        for g in range(4):
+            lb = lg[r, 4 * g : 4 * g + 4].reshape(128, S)
+            u = dot_nt(rp[...], lb).astype(BF16)
+            at = (r * 4 + g) * 16
+            for b in range(32):
+                lhs2[at : at + 16, b * 128 : (b + 1) * 128] = u[b * 16 : (b + 1) * 16]
     landed(rg.at[pl.ds(0, LINE - 1)], ssem.at[4])
-    for g in range(8):
-        lb = lg[2 * g : 2 * g + 2].reshape(128, S)
-        u = dot_nt(rp[...], lb).astype(BF16)
-        for b in range(32):
-            lhs2[g * 16 : (g + 1) * 16, b * 128 : (b + 1) * 128] = u[b * 16 : (b + 1) * 16]
     block = dot(lhs2[...], bd[...])
     for u in range(PLANE):
         for r in range(2):
-            at = 2 * (u % 2) + r
-            osend[u, r] = block[
-                (u // 2) * 16 : (u // 2 + 1) * 16, at * 128 : (at + 1) * 128
-            ].astype(BF16)
+            row, at = (r * 4 + u // 4) * 16, u % 4
+            osend[u, r] = block[row : row + 16, at * 128 : (at + 1) * 128].astype(BF16)
     og[my_u] = osend[my_u]
 
-    def give_back(i, _):
-        to_u = lax.rem(my_u + i, PLANE)
+    for n in PLANE_FAR_FIRST:
+        to_u = lax.rem(x_at + n // 4, 4) * 4 + lax.rem(y_at + n % 4, 4)
         send(osend.at[to_u], og.at[my_u], ssem.at[5], rsem.at[5], to_u * LINE + my_v)
-        return 0
-
-    lax.fori_loop(1, PLANE, give_back, 0)
     landed(og.at[pl.ds(0, PLANE - 1)], rsem.at[5])
     landed(og.at[pl.ds(0, PLANE - 1)], ssem.at[5])
     for r in range(2):
@@ -308,7 +323,7 @@
         pnow[r] = pair[r] + delta * cnt[r]
 
     lanes = lax.broadcasted_iota(jnp.int32, (1, S), 1)
-    am = amino[...].astype(F32)[None, :]
+    am = amino[...].astype(F32)
     for w in range(2):
         for r in range(2):
             x = norm(pnow[r], g_in[w : w + 1, :]).astype(BF16)
@@ -370,9 +385,32 @@
                     pnow[r, rows, :] = new
                 else:
                     pair_out[r, rows, :] = new
+            if w == 1:
+                pltpu.make_async_copy(pair_out.at[r], outs[1].at[r], osem.at[1 + r]).start()
+    pltpu.make_async_copy(msa_out, outs[0], osem.at[0]).wait()
+    for r in range(2):
+        pltpu.make_async_copy(pair_out.at[r], outs[1].at[r], osem.at[1 + r]).wait()
+
+
+def copied(a, b, a_out, b_out, a_here, b_here, sems):
+    moves = []
+    for n in range(4):
+        part = pl.ds(n * 256, 256)
+        moves.append((a.at[part], a_here.at[part], a_out.at[part]))
+    for n in range(2):
+        moves.append((b.at[n], b_here.at[n], b_out.at[n]))
+    for n, (src, here, _) in enumerate(moves):
+        pltpu.make_async_copy(src, here, sems.at[n]).start()
+    for n, (src, here, dst) in enumerate(moves):
+        pltpu.make_async_copy(src, here, sems.at[n]).wait()
+        pltpu.make_async_copy(here, dst, sems.at[6 + n]).start()
+    for n, (_, here, dst) in enumerate(moves):
+        pltpu.make_async_copy(here, dst, sems.at[6 + n]).wait()
 
 
 SCRATCH = [
+    ((S * 4, 128), F32),
+    ((2, S, CZ), F32),
     ((BA, 128), BF16),
     ((BB, 128), BF16),
     ((2, N // 2, BA, 128), BF16),
@@ -393,10 +431,10 @@
     ((S, S), F32),
     ((S, S), BF16),
     ((2, S, CZ), F32),
-    ((64, S), BF16),
-    ((64, S), BF16),
-    ((PLANE, 64, S), BF16),
-    ((LINE, 64, S), BF16),
+    ((2, 32, S), BF16),
+    ((2, 32, S), BF16),
+    ((2, PLANE, 32, S), BF16),
+    ((LINE, 2, 32, S), BF16),
     ((2, 512, 128), F32),
     ((512, S), BF16),
     ((128, 4096), BF16),
@@ -418,21 +456,34 @@
 
 
 def shards(*args):
-    vmem = pl.BlockSpec(memory_space=pltpu.VMEM)
+    args = [a.reshape(1, -1) if a.ndim == 1 else a for a in args]
+    for n in (9, 15):
+        args[n] = args[n].T
+    anywhere = pl.BlockSpec(memory_space=pl.ANY)
+    results = (
+        jax.ShapeDtypeStruct((S * 4, 128), F32),
+        jax.ShapeDtypeStruct((2, S, CZ), F32),
+    )
     flat, pair = pl.pallas_call(
         body,
-        out_shape=(
-            jax.ShapeDtypeStruct((S * 4, 128), F32),
-            jax.ShapeDtypeStruct((2, S, CZ), F32),
-        ),
-        in_specs=[vmem] * len(args),
-        out_specs=(vmem, vmem),
-        scratch_shapes=[pltpu.VMEM(shape, dtype) for shape, dtype in SCRATCH]
-        + [pltpu.SemaphoreType.DMA((12,)), pltpu.SemaphoreType.DMA((12,))],
+        out_shape=results,
+        in_specs=[anywhere] * N_IN,
+        out_specs=(anywhere, anywhere),
+        scratch_shapes=[pltpu.VMEM(a.shape, a.dtype) for a in args]
+        + [pltpu.VMEM(shape, dtype) for shape, dtype in SCRATCH]
+        + [pltpu.SemaphoreType.DMA((n,)) for n in (13, 13, N_IN, 3)],
         compiler_params=pltpu.CompilerParams(
             collective_id=0, has_side_effects=True, vmem_limit_bytes=60 << 20
         ),
-    )(*args[:9], args[9].T, *args[10:15], args[15].T, *args[16:])
+    )(*args)
+    flat, pair = pl.pallas_call(
+        copied,
+        out_shape=results,
+        in_specs=[anywhere] * 2,
+        out_specs=(anywhere, anywhere),
+        scratch_shapes=[pltpu.VMEM(a.shape, a.dtype) for a in results]
+        + [pltpu.SemaphoreType.DMA((12,))],
+    )(flat, pair)
     return flat.reshape(S, 2, 2, 128).transpose(0, 2, 1, 3).reshape(S, 2, H), pair
 
 

time: 85.6 us -> 81.3 us (0.950)
  local copies, waits for them, and re-layouts: 2.76 us -> 0 us
  Pallas kernels: 82 us -> 80.3 us
    unnamed x4 -> x0, local copies, waits for them, and re-layouts: 2.76 us -> none
    pallas_call x1 -> x2, Pallas kernels: 82 us -> 80.3 us  [the longest x1 78.4 us: shards(): pl.pallas_call(body, out_shape=results, in_specs=[anywhere] * N_IN, out_s...]
where the time goes in v2:
time: 81.3 us; the launch traced here: 81.1 us
  Pallas kernels  80.3 us (99%)
    pallas_call x1, Pallas kernels, shards(): pl.pallas_call(body, out_shape=results, in_specs=[anywhere] * N_IN, out_s...  78.4 us
    pallas_call x1, Pallas kernels, shards(): pl.pallas_call(copied, out_shape=results, in_specs=[anywhere] * 2, out_sp...  1.97 us

profile of v2, /device:TPU:1, one launch (start us, length us, event | category | flops | bytes accessed | tf_op | source)
XLA Modules:
  0.0 81.1 jit_solution(1006020986282542057)
XLA Ops:
  0.6 78.4 %shard_map.221 = (f32[1024,128]{1,0:T(8,128)}, f32[2,256,128]{2,1,0:T(8,128)}) custom-call(f32[2,256,256]{2,1,0:T(8,128)} %refs_0_.1, f32[2,256,128]{2,1,0:T(8,128)} %refs_1_.1, s32[2,256]{1,0:T(2,128)} %refs_2_.1, s32[1,256]{1,0:T(1,128)} %bitcast.14, f32[1,256]{1,0:T(1,128)} %bitcast.15, bf16[256,256]{1,0:T(8,128)(2,1)} %refs_5_.1, ...), custom_call_target="tpu_custom_call" | custom-call | tf_op jit(solution)/shard_map/pallas_call | solution.py:467
  79.0 2.0 %shard_map.222 = (f32[1024,128]{1,0:T(8,128)}, f32[2,256,128]{2,1,0:T(8,128)}) custom-call(f32[1024,128]{1,0:T(8,128)} %get-tuple-element.6.a, f32[2,256,128]{2,1,0:T(8,128)} %get-tuple-element.7.b), custom_call_target="tpu_custom_call" | custom-call | tf_op jit(solution)/shard_map/pallas_call | solution.py:479

commit v3 on v2

--- a/solution.py
+++ b/solution.py
@@ -81,15 +81,16 @@
 def body(*refs):
     ins, outs, refs = refs[:N_IN], refs[N_IN : N_IN + 2], refs[N_IN + 2 :]
     here, refs = refs[:N_IN], refs[N_IN:]
+    msa_out, pair_out = outs
     (
         msa, pair, pres, amino, g_row, wq1, wkvg1, wo1, g_bias, wb, g_col,
         wq2, wkvg2, wo2, g_opm, wlr, wfin, g_in, wproj, wgate, g_mid, wout,
     ) = here
     (
-        msa_out, pair_out, bsa, bsb, ba, bb, wa, wb32, xn, msah, q, kt, vbd, prob, gate, a32,
+        bsa, bsb, ba, bb, wa, wb32, xn, msah, q, kt, vbd, prob, gate, a32,
         asend, arecv, xc, pm, pmt, cnt, lsend, rsend, lg, rg, r32, rp, lhs2, bd, osend, og,
         wt, gmt, pad, t32, tsend, trecv, tgate, p32, psend, precv, pnow,
-        ssem, rsem, isem, osem,
+        ssem, rsem, isem,
     ) = refs
     me = lax.axis_index("dap")
     core = lax.rem(me, 2)
@@ -111,6 +112,16 @@
             if not here:
                 yield there * 2 + core
             yield there * 2 + 1 - core
+
+    def plane():
+        for n in PLANE_FAR_FIRST:
+            yield lax.rem(x_at + n // 4, 4) * 4 + lax.rem(y_at + n % 4, 4)
+
+    def line():
+        for n in (2, 1, 3, 0):
+            if n:
+                yield lax.rem(z_at + n, 4) * 2 + core
+            yield lax.rem(z_at + n, 4) * 2 + 1 - core
 
     barrier = pltpu.get_barrier_semaphore()
     for to in peers():
@@ -276,51 +287,49 @@
         projected = dot_nt(wlr[...], xb) * mine[r : r + 1, :]
         lsend[r] = projected[0:32].astype(BF16)
         rsend[r] = projected[32:64].astype(BF16)
-        lg[r, my_u] = lsend[r]
+        rg[r, my_u] = rsend[r]
         if r == 1:
-            rg[my_v] = rsend[...]
-            for n in range(1, LINE):
-                send(
-                    rsend, rg.at[my_v], ssem.at[4], rsem.at[4],
-                    my_u * LINE + lax.rem(my_v + n, LINE),
-                )
-        for n in PLANE_FAR_FIRST:
-            to = lax.rem(x_at + n // 4, 4) * 32 + lax.rem(y_at + n % 4, 4) * 8 + my_v
-            send(lsend.at[r], lg.at[r, my_u], ssem.at[3 + 9 * r], rsem.at[3 + 9 * r], to)
-    pltpu.make_async_copy(msa_out, outs[0], osem.at[0]).start()
-
-    landed(rg.at[pl.ds(0, LINE - 1)], rsem.at[4])
-    for c in range(2):
-        r32[c] = rg[:, :, :, c * 128 : (c + 1) * 128].astype(F32).reshape(512, 128)
-    for b in range(32):
-        rp[b * 16 : (b + 1) * 16, :] = jnp.concatenate(
-            [r32[c, pl.ds(b, 16, stride=32), :] for c in range(2)], axis=1
-        ).astype(BF16)
+            lg[my_v] = lsend[...]
+            for to_v in line():
+                send(lsend, lg.at[my_v], ssem.at[4], rsem.at[4], my_u * LINE + to_v)
+        for to_u in plane():
+            to = to_u * LINE + my_v
+            send(rsend.at[r], rg.at[r, my_u], ssem.at[3 + 9 * r], rsem.at[3 + 9 * r], to)
+
     for r in range(2):
         for sems in (rsem, ssem):
-            landed(lg.at[0, pl.ds(0, PLANE - 1)], sems.at[3 + 9 * r])
+            landed(rg.at[0, pl.ds(0, PLANE - 1)], sems.at[3 + 9 * r])
+        for c in range(2):
+            r32[c] = rg[r, :, :, c * 128 : (c + 1) * 128].astype(F32).reshape(512, 128)
+        for b in range(32):
+            rp[r, b * 16 : (b + 1) * 16, :] = jnp.concatenate(
+                [r32[c, pl.ds(b, 16, stride=32), :] for c in range(2)], axis=1
+            ).astype(BF16)
+        if r == 0:
+            for sems in (rsem, ssem):
+                landed(lg.at[pl.ds(0, LINE - 1)], sems.at[4])
         for g in range(4):
-            lb = lg[r, 4 * g : 4 * g + 4].reshape(128, S)
-            u = dot_nt(rp[...], lb).astype(BF16)
-            at = (r * 4 + g) * 16
+            lb = lg[2 * g : 2 * g + 2].reshape(128, S)
+            u = dot_nt(rp[r], lb).astype(BF16)
+            at = g * 32 + r * 16
             for b in range(32):
                 lhs2[at : at + 16, b * 128 : (b + 1) * 128] = u[b * 16 : (b + 1) * 16]
-    landed(rg.at[pl.ds(0, LINE - 1)], ssem.at[4])
     block = dot(lhs2[...], bd[...])
-    for u in range(PLANE):
-        for r in range(2):
-            row, at = (r * 4 + u // 4) * 16, u % 4
-            osend[u, r] = block[row : row + 16, at * 128 : (at + 1) * 128].astype(BF16)
-    og[my_u] = osend[my_u]
-
-    for n in PLANE_FAR_FIRST:
-        to_u = lax.rem(x_at + n // 4, 4) * 4 + lax.rem(y_at + n % 4, 4)
-        send(osend.at[to_u], og.at[my_u], ssem.at[5], rsem.at[5], to_u * LINE + my_v)
-    landed(og.at[pl.ds(0, PLANE - 1)], rsem.at[5])
-    landed(og.at[pl.ds(0, PLANE - 1)], ssem.at[5])
-    for r in range(2):
-        delta = og[:, r].astype(F32).reshape(S, CZ)
-        pnow[r] = pair[r] + delta * cnt[r]
+    for to_v in range(LINE):
+        for r in range(2):
+            row, at = (to_v // 2) * 32, (to_v % 2) * 2 + r
+            osend[to_v, r] = block[row : row + 32, at * 128 : (at + 1) * 128].astype(BF16)
+    og[my_v] = osend[my_v]
+    for to_v in line():
+        send(osend.at[to_v], og.at[my_v], ssem.at[5], rsem.at[5], my_u * LINE + to_v)
+    for sems in (rsem, ssem):
+        landed(og.at[pl.ds(0, LINE - 1)], sems.at[5])
+    for r in range(2):
+        for from_v in range(LINE):
+            for half in range(2):
+                rows = pl.ds(2 * from_v + half, 16, stride=16)
+                delta = og[from_v, r, half * 16 : (half + 1) * 16].astype(F32)
+                pnow[r, rows, :] = pair[r, rows, :] + delta * cnt[r, rows, :]
 
     lanes = lax.broadcasted_iota(jnp.int32, (1, S), 1)
     am = amino[...].astype(F32)
@@ -385,32 +394,16 @@
                     pnow[r, rows, :] = new
                 else:
                     pair_out[r, rows, :] = new
-            if w == 1:
-                pltpu.make_async_copy(pair_out.at[r], outs[1].at[r], osem.at[1 + r]).start()
-    pltpu.make_async_copy(msa_out, outs[0], osem.at[0]).wait()
-    for r in range(2):
-        pltpu.make_async_copy(pair_out.at[r], outs[1].at[r], osem.at[1 + r]).wait()
-
-
-def copied(a, b, a_out, b_out, a_here, b_here, sems):
-    moves = []
-    for n in range(4):
-        part = pl.ds(n * 256, 256)
-        moves.append((a.at[part], a_here.at[part], a_out.at[part]))
-    for n in range(2):
-        moves.append((b.at[n], b_here.at[n], b_out.at[n]))
-    for n, (src, here, _) in enumerate(moves):
-        pltpu.make_async_copy(src, here, sems.at[n]).start()
-    for n, (src, here, dst) in enumerate(moves):
-        pltpu.make_async_copy(src, here, sems.at[n]).wait()
-        pltpu.make_async_copy(here, dst, sems.at[6 + n]).start()
-    for n, (_, here, dst) in enumerate(moves):
-        pltpu.make_async_copy(here, dst, sems.at[6 + n]).wait()
+
+
+def copied(a, b, a_out, b_out, sems):
+    pltpu.make_async_copy(a, a_out, sems.at[0]).start()
+    pltpu.make_async_copy(b, b_out, sems.at[1]).start()
+    pltpu.make_async_copy(a, a_out, sems.at[0]).wait()
+    pltpu.make_async_copy(b, b_out, sems.at[1]).wait()
 
 
 SCRATCH = [
-    ((S * 4, 128), F32),
-    ((2, S, CZ), F32),
     ((BA, 128), BF16),
     ((BB, 128), BF16),
     ((2, N // 2, BA, 128), BF16),
@@ -433,14 +426,14 @@
     ((2, S, CZ), F32),
     ((2, 32, S), BF16),
     ((2, 32, S), BF16),
+    ((LINE, 2, 32, S), BF16),
     ((2, PLANE, 32, S), BF16),
-    ((LINE, 2, 32, S), BF16),
     ((2, 512, 128), F32),
-    ((512, S), BF16),
+    ((2, 512, S), BF16),
     ((128, 4096), BF16),
     ((4096, 512), BF16),
-    ((PLANE, 2, 16, 128), BF16),
-    ((PLANE, 2, 16, 128), BF16),
+    ((LINE, 2, 32, 128), BF16),
+    ((LINE, 2, 32, 128), BF16),
     ((2, 512, 128), BF16),
     ((2, CZ, CZ), F32),
     ((BA + BB, 128), F32),
@@ -460,18 +453,19 @@
     for n in (9, 15):
         args[n] = args[n].T
     anywhere = pl.BlockSpec(memory_space=pl.ANY)
+    local = pl.BlockSpec(memory_space=pltpu.VMEM)
     results = (
         jax.ShapeDtypeStruct((S * 4, 128), F32),
         jax.ShapeDtypeStruct((2, S, CZ), F32),
     )
     flat, pair = pl.pallas_call(
         body,
-        out_shape=results,
+        out_shape=tuple(pltpu.VMEM(a.shape, a.dtype) for a in results),
         in_specs=[anywhere] * N_IN,
-        out_specs=(anywhere, anywhere),
+        out_specs=(local, local),
         scratch_shapes=[pltpu.VMEM(a.shape, a.dtype) for a in args]
         + [pltpu.VMEM(shape, dtype) for shape, dtype in SCRATCH]
-        + [pltpu.SemaphoreType.DMA((n,)) for n in (13, 13, N_IN, 3)],
+        + [pltpu.SemaphoreType.DMA((n,)) for n in (13, 13, N_IN)],
         compiler_params=pltpu.CompilerParams(
             collective_id=0, has_side_effects=True, vmem_limit_bytes=60 << 20
         ),
@@ -479,11 +473,10 @@
     flat, pair = pl.pallas_call(
         copied,
         out_shape=results,
-        in_specs=[anywhere] * 2,
+        in_specs=[local] * 2,
         out_specs=(anywhere, anywhere),
-        scratch_shapes=[pltpu.VMEM(a.shape, a.dtype) for a in results]
-        + [pltpu.SemaphoreType.DMA((12,))],
-    )(flat, pair)
+        scratch_shapes=[pltpu.SemaphoreType.DMA((2,))],
+    )(*(pltpu.with_memory_space_constraint(a, pltpu.VMEM) for a in (flat, pair)))
     return flat.reshape(S, 2, 2, 128).transpose(0, 2, 1, 3).reshape(S, 2, H), pair
 
 

time: 81.3 us -> 78.7 us (0.968)
  Pallas kernels: 80.3 us -> 77.8 us
    pallas_call x2, Pallas kernels: 80.3 us -> 77.8 us  [the longest x1 76.9 us: shards(): pl.pallas_call(body, out_shape=tuple((pltpu.VMEM(a.shape, a.dtype) for a...]
where the time goes in v3:
time: 78.7 us; the launch traced here: 78.6 us
  Pallas kernels  77.8 us (99%)
  between operations  0.81 us (1%)
    pallas_call x1, Pallas kernels, shards(): pl.pallas_call(body, out_shape=tuple((pltpu.VMEM(a.shape, a.dtype) for a...  76.9 us

profile of v3, /device:TPU:1, one launch (start us, length us, event | category | flops | bytes accessed | tf_op | source)
XLA Modules:
  0.0 78.6 jit_solution(6974662819990352171)
XLA Ops:
  0.6 76.9 %shard_map.221 = (f32[1024,128]{1,0:T(8,128)S(1)}, f32[2,256,128]{2,1,0:T(8,128)S(1)}) custom-call(f32[2,256,256]{2,1,0:T(8,128)} %refs_0_.1, f32[2,256,128]{2,1,0:T(8,128)} %refs_1_.1, s32[2,256]{1,0:T(2,128)} %refs_2_.1, s32[1,256]{1,0:T(1,128)} %bitcast.14, f32[1,256]{1,0:T(1,128)} %bitcast.15, bf16[256,256]{1,0:T(8,128)(2,1)} %refs_5_.1, ...), custom_call_target="tpu_custom_call" | custom-call | tf_op jit(solution)/shard_map/pallas_call | solution.py:461
  77.5 0.9 %shard_map.222 = (f32[1024,128]{1,0:T(8,128)}, f32[2,256,128]{2,1,0:T(8,128)}) custom-call(f32[1024,128]{1,0:T(8,128)S(1)} %get-tuple-element.6.a, f32[2,256,128]{2,1,0:T(8,128)S(1)} %get-tuple-element.7.b), custom_call_target="tpu_custom_call" | custom-call | tf_op jit(solution)/shard_map/pallas_call | solution.py:473

commit v4 on v3

--- a/solution.py
+++ b/solution.py
@@ -15,7 +15,7 @@
 WIDTH = 32
 PLANE = 16
 LINE = 8
-BA, BB = 16, 24
+BA, BB, BC = 16, 16, 8
 N_IN = 22
 HOPS = (0, 1, 2, 1)
 FAR_FIRST = sorted(
@@ -68,14 +68,10 @@
         vbd[t, h * S : (h + 1) * S, :] = v * head_lanes(h)
 
 
-def attend_head(h, t, q, kt, prob, bias, pen):
-    scores = dot(q[t] * head_lanes(h), kt[t])
-    if bias is not None:
-        scores = scores + bias
-    scores = scores + pen
+def probabilities(scores):
     top = jnp.max(scores, axis=-1, keepdims=True)
     e = jnp.exp(scores - top)
-    prob[t, :, h * S : (h + 1) * S] = (e * (1.0 / jnp.sum(e, axis=-1, keepdims=True))).astype(BF16)
+    return (e * (1.0 / jnp.sum(e, axis=-1, keepdims=True))).astype(BF16)
 
 
 def body(*refs):
@@ -87,7 +83,7 @@
         wq2, wkvg2, wo2, g_opm, wlr, wfin, g_in, wproj, wgate, g_mid, wout,
     ) = here
     (
-        bsa, bsb, ba, bb, wa, wb32, xn, msah, q, kt, vbd, prob, gate, a32,
+        bsa, bsb, bsc, ba, bb, bc, wa, wb32, wc, raw, tx, xn, msah, q, kt, vbd, prob, gate, a32,
         asend, arecv, xc, pm, pmt, cnt, lsend, rsend, lg, rg, r32, rp, lhs2, bd, osend, og,
         wt, gmt, pad, t32, tsend, trecv, tgate, p32, psend, precv, pnow,
         ssem, rsem, isem,
@@ -149,12 +145,14 @@
     presence = pres[...].astype(F32)
     for r in range(2):
         for j in range(2):
-            at = BA + 16 + r * 2 + j
+            at = BA + BB + r * 2 + j
             pad[at : at + 1, :] = presence[r : r + 1, j * 128 : (j + 1) * 128]
     bsa[...] = pad[0:BA, :].astype(BF16)
     bsb[...] = pad[BA : BA + BB, :].astype(BF16)
+    bsc[...] = pad[BA + BB :, :].astype(BF16)
     ba[core, chip] = bsa[...]
     bb[core, chip] = bsb[...]
+    bc[core, chip] = bsc[...]
 
     arrived(0, 4, 5, 6)
     for s in range(2):
@@ -188,25 +186,34 @@
             bd[b * 128 + i * 32 : b * 128 + (i + 1) * 32, i * 128 : (i + 1) * 128] = part
 
     pl.semaphore_wait(barrier, N - 1)
-    for src, dst, sem in ((bsa, ba, 0), (bsb, bb, 10)):
+    for src, dst, sem in ((bsa, ba, 0), (bsb, bb, 10), (bsc, bc, 13)):
         for there, here in chips():
             if not here:
                 send(src, dst.at[core, chip], ssem.at[sem], rsem.at[sem], there * 2 + core)
 
     pens = [PENALTY * (presence[s : s + 1, :] - 1.0) for s in range(2)]
+    for h in range(HEADS):
+        for t in range(2):
+            raw[t, :, h * S : (h + 1) * S] = dot(q[t] * head_lanes(h), kt[t])
+
     halves = ((ba, wa, BA, 0), (bb, wb32, BB, 10))
+
+    sent = []
 
     def swap(dst, sem):
         landed(dst.at[0, pl.ds(0, N // 2 - 1)], rsem.at[sem])
         send(dst.at[core], dst.at[core], ssem.at[sem + 1], rsem.at[sem + 1], partner)
 
+    def swapped(dst, wide, rows_of, sem):
+        landed(dst.at[0], rsem.at[sem + 1])
+        sent.append((dst.at[0, pl.ds(0, N // 2 - 1)], sem))
+        sent.append((dst.at[0], sem + 1))
+        for d in range(N):
+            wide[d * rows_of : (d + 1) * rows_of, :] = dst[d % 2, d // 2].astype(F32)
+
     swap(ba, 0)
     for half, (dst, wide, rows_of, sem) in enumerate(halves):
-        landed(dst.at[0], rsem.at[sem + 1])
-        landed(dst.at[0, pl.ds(0, N // 2 - 1)], ssem.at[sem])
-        landed(dst.at[0], ssem.at[sem + 1])
-        for d in range(N):
-            wide[d * rows_of : (d + 1) * rows_of, :] = dst[d % 2, d // 2].astype(F32)
+        swapped(dst, wide, rows_of, sem)
         for h in range(4):
             bias = jnp.concatenate(
                 [
@@ -222,9 +229,11 @@
                 axis=0,
             )
             for t in range(2):
-                attend_head(half * 4 + h, t, q, kt, prob, bias, pens[t])
+                at = slice((half * 4 + h) * S, (half * 4 + h + 1) * S)
+                prob[t, :, at] = probabilities(raw[t, :, at] + bias + pens[t])
             if half == 0 and h == 1:
                 swap(bb, 10)
+    swap(bc, 13)
     for s in range(2):
         y = (dot(prob[s], vbd[s]) * gate[s]).astype(BF16)
         step = dot(y, wo1[...])
@@ -241,14 +250,15 @@
 
     def received(src, dst, sem):
         landed(dst.at[pl.ds(0, N - 1)], rsem.at[sem])
-        landed(src.at[pl.ds(0, N - 1)], ssem.at[sem])
+        sent.append((src.at[pl.ds(0, N - 1)], sem))
 
     exchange(asend, arecv, 2)
 
+    swapped(bc, wc, BC, 13)
     for s in range(2):
         for j in range(2):
-            pm[s * 128 : (s + 1) * 128, j * 128 : (j + 1) * 128] = wb32[
-                pl.ds(16 + s * 2 + j, 128, stride=BB), :
+            pm[s * 128 : (s + 1) * 128, j * 128 : (j + 1) * 128] = wc[
+                pl.ds(s * 2 + j, 128, stride=BC), :
             ]
     pmt[...] = pm[...].T.astype(BF16)
     own = lax.broadcasted_iota(jnp.int32, (16, S), 0) + 2 * me
@@ -275,14 +285,10 @@
         gate[r] = jax.nn.sigmoid(dot(xb, wkvg2[:, 2 * H :]))
     for r in range(2):
         for h in range(HEADS):
-            attend_head(h, r, q, kt, prob, None, PENALTY * (mine[r : r + 1, :] - 1.0))
+            scores = dot(q[r] * head_lanes(h), kt[r]) + PENALTY * (mine[r : r + 1, :] - 1.0)
+            prob[r, :, h * S : (h + 1) * S] = probabilities(scores)
         y = (dot(prob[r], vbd[r]) * gate[r]).astype(BF16)
         done = xc[r] + dot(y, wo2[...])
-        for s in range(2):
-            for c in range(2):
-                msa_out[pl.ds(s * 4 + c * 2 + r, 128, stride=8), :] = done[
-                    s * 128 : (s + 1) * 128, c * 128 : (c + 1) * 128
-                ]
         xb = norm(done, g_opm[...]).astype(BF16)
         projected = dot_nt(wlr[...], xb) * mine[r : r + 1, :]
         lsend[r] = projected[0:32].astype(BF16)
@@ -295,10 +301,15 @@
         for to_u in plane():
             to = to_u * LINE + my_v
             send(rsend.at[r], rg.at[r, my_u], ssem.at[3 + 9 * r], rsem.at[3 + 9 * r], to)
-
-    for r in range(2):
-        for sems in (rsem, ssem):
-            landed(rg.at[0, pl.ds(0, PLANE - 1)], sems.at[3 + 9 * r])
+        for s in range(2):
+            for c in range(2):
+                msa_out[pl.ds(s * 4 + c * 2 + r, 128, stride=8), :] = done[
+                    s * 128 : (s + 1) * 128, c * 128 : (c + 1) * 128
+                ]
+
+    for r in range(2):
+        landed(rg.at[0, pl.ds(0, PLANE - 1)], rsem.at[3 + 9 * r])
+        sent.append((rg.at[0, pl.ds(0, PLANE - 1)], 3 + 9 * r))
         for c in range(2):
             r32[c] = rg[r, :, :, c * 128 : (c + 1) * 128].astype(F32).reshape(512, 128)
         for b in range(32):
@@ -306,8 +317,8 @@
                 [r32[c, pl.ds(b, 16, stride=32), :] for c in range(2)], axis=1
             ).astype(BF16)
         if r == 0:
-            for sems in (rsem, ssem):
-                landed(lg.at[pl.ds(0, LINE - 1)], sems.at[4])
+            landed(lg.at[pl.ds(0, LINE - 1)], rsem.at[4])
+            sent.append((lg.at[pl.ds(0, LINE - 1)], 4))
         for g in range(4):
             lb = lg[2 * g : 2 * g + 2].reshape(128, S)
             u = dot_nt(rp[r], lb).astype(BF16)
@@ -322,8 +333,8 @@
     og[my_v] = osend[my_v]
     for to_v in line():
         send(osend.at[to_v], og.at[my_v], ssem.at[5], rsem.at[5], my_u * LINE + to_v)
-    for sems in (rsem, ssem):
-        landed(og.at[pl.ds(0, LINE - 1)], sems.at[5])
+    landed(og.at[pl.ds(0, LINE - 1)], rsem.at[5])
+    sent.append((og.at[pl.ds(0, LINE - 1)], 5))
     for r in range(2):
         for from_v in range(LINE):
             for half in range(2):
@@ -346,10 +357,12 @@
                     t32[pl.ds(side * 4 + r * 2 + j, 128, stride=8), :] = val[
                         :, j * 128 : (j + 1) * 128
                     ]
-            tgate[r] = jax.nn.sigmoid(dot(x, wgate[w]))
+            tx[r] = x
         tsend[w] = t32[...].reshape(N, 8, 128).astype(BF16)
         trecv[w, me] = tsend[w, me]
         exchange(tsend.at[w], trecv.at[w], 6 + 2 * w)
+        for r in range(2):
+            tgate[r] = jax.nn.sigmoid(dot(tx[r], wgate[w]))
         received(tsend.at[w], trecv.at[w], 6 + 2 * w)
         t32[...] = trecv[w].astype(F32).reshape(N * 8, 128)
         sides = []
@@ -395,6 +408,9 @@
                 else:
                     pair_out[r, rows, :] = new
 
+    for like, sem in sent:
+        landed(like, ssem.at[sem])
+
 
 def copied(a, b, a_out, b_out, sems):
     pltpu.make_async_copy(a, a_out, sems.at[0]).start()
@@ -406,10 +422,15 @@
 SCRATCH = [
     ((BA, 128), BF16),
     ((BB, 128), BF16),
+    ((BC, 128), BF16),
     ((2, N // 2, BA, 128), BF16),
     ((2, N // 2, BB, 128), BF16),
+    ((2, N // 2, BC, 128), BF16),
     ((N * BA, 128), F32),
     ((N * BB, 128), F32),
+    ((N * BC, 128), F32),
+    ((2, S, HEADS * S), F32),
+    ((2, S, CZ), BF16),
     ((2, S, 128), F32),
     ((2, 2, S, 128), F32),
     ((2, S, H), BF16),
@@ -436,7 +457,7 @@
     ((LINE, 2, 32, 128), BF16),
     ((2, 512, 128), BF16),
     ((2, CZ, CZ), F32),
-    ((BA + BB, 128), F32),
+    ((BA + BB + BC, 128), F32),
     ((N * 8, 128), F32),
     ((2, N, 8, 128), BF16),
     ((2, N, 8, 128), BF16),
@@ -465,7 +486,7 @@
         out_specs=(local, local),
         scratch_shapes=[pltpu.VMEM(a.shape, a.dtype) for a in args]
         + [pltpu.VMEM(shape, dtype) for shape, dtype in SCRATCH]
-        + [pltpu.SemaphoreType.DMA((n,)) for n in (13, 13, N_IN)],
+        + [pltpu.SemaphoreType.DMA((n,)) for n in (15, 15, N_IN)],
         compiler_params=pltpu.CompilerParams(
             collective_id=0, has_side_effects=True, vmem_limit_bytes=60 << 20
         ),

time: 78.7 us -> 77.3 us (0.982)
  Pallas kernels: 77.8 us -> 76.4 us
    pallas_call x1, Pallas kernels: 76.9 us -> 75.5 us  [shards(): pl.pallas_call(body, out_shape=tuple((pltpu.VMEM(a.shape, a.dtype) for a...]
where the time goes in v4:
time: 77.3 us; the launch traced here: 77.2 us
  Pallas kernels  76.4 us (99%)
  between operations  0.81 us (1%)
    pallas_call x1, Pallas kernels, shards(): pl.pallas_call(body, out_shape=tuple((pltpu.VMEM(a.shape, a.dtype) for a...  75.5 us

profile of v4, /device:TPU:1, one launch (start us, length us, event | category | flops | bytes accessed | tf_op | source)
XLA Modules:
  0.0 77.2 jit_solution(13936104015172946122)
XLA Ops:
  0.6 75.5 %shard_map.221 = (f32[1024,128]{1,0:T(8,128)S(1)}, f32[2,256,128]{2,1,0:T(8,128)S(1)}) custom-call(f32[2,256,256]{2,1,0:T(8,128)} %refs_0_.1, f32[2,256,128]{2,1,0:T(8,128)} %refs_1_.1, s32[2,256]{1,0:T(2,128)} %refs_2_.1, s32[1,256]{1,0:T(1,128)} %bitcast.14, f32[1,256]{1,0:T(1,128)} %bitcast.15, bf16[256,256]{1,0:T(8,128)(2,1)} %refs_5_.1, ...), custom_call_target="tpu_custom_call" | custom-call | tf_op jit(solution)/shard_map/pallas_call | solution.py:482
  76.2 0.9 %shard_map.222 = (f32[1024,128]{1,0:T(8,128)}, f32[2,256,128]{2,1,0:T(8,128)}) custom-call(f32[1024,128]{1,0:T(8,128)S(1)} %get-tuple-element.6.a, f32[2,256,128]{2,1,0:T(8,128)S(1)} %get-tuple-element.7.b), custom_call_target="tpu_custom_call" | custom-call | tf_op jit(solution)/shard_map/pallas_call | solution.py:494

commit v5 on v4

--- a/solution.py
+++ b/solution.py
@@ -283,7 +283,6 @@
         kt[r] = dot(xb, wkvg2[:, 0:H]).T.astype(BF16)
         spread_heads(dot(xb, wkvg2[:, H : 2 * H]).astype(BF16), vbd, r)
         gate[r] = jax.nn.sigmoid(dot(xb, wkvg2[:, 2 * H :]))
-    for r in range(2):
         for h in range(HEADS):
             scores = dot(q[r] * head_lanes(h), kt[r]) + PENALTY * (mine[r : r + 1, :] - 1.0)
             prob[r, :, h * S : (h + 1) * S] = probabilities(scores)

time: 77.3 us -> 77.3 us (level)
  no operation moved by 1% of the time
where the time goes in v5:
time: 77.3 us; the launch traced here: 77.2 us
  Pallas kernels  76.4 us (99%)
  between operations  0.81 us (1%)
    pallas_call x1, Pallas kernels, shards(): pl.pallas_call(body, out_shape=tuple((pltpu.VMEM(a.shape, a.dtype) for a...  75.5 us

profile of v5, /device:TPU:1, one launch (start us, length us, event | category | flops | bytes accessed | tf_op | source)
XLA Modules:
  0.0 77.2 jit_solution(1446768829430446211)
XLA Ops:
  0.6 75.5 %shard_map.221 = (f32[1024,128]{1,0:T(8,128)S(1)}, f32[2,256,128]{2,1,0:T(8,128)S(1)}) custom-call(f32[2,256,256]{2,1,0:T(8,128)} %refs_0_.1, f32[2,256,128]{2,1,0:T(8,128)} %refs_1_.1, s32[2,256]{1,0:T(2,128)} %refs_2_.1, s32[1,256]{1,0:T(1,128)} %bitcast.14, f32[1,256]{1,0:T(1,128)} %bitcast.15, bf16[256,256]{1,0:T(8,128)(2,1)} %refs_5_.1, ...), custom_call_target="tpu_custom_call" | custom-call | tf_op jit(solution)/shard_map/pallas_call | solution.py:481
  76.1 0.9 %shard_map.222 = (f32[1024,128]{1,0:T(8,128)}, f32[2,256,128]{2,1,0:T(8,128)}) custom-call(f32[1024,128]{1,0:T(8,128)S(1)} %get-tuple-element.6.a, f32[2,256,128]{2,1,0:T(8,128)S(1)} %get-tuple-element.7.b), custom_call_target="tpu_custom_call" | custom-call | tf_op jit(solution)/shard_map/pallas_call | solution.py:493
